TPU v7x, 32 devices: a whole 2x2x4 slice. The times are simulated.
32 devices in a mesh: group: 4 (over y, x), hash: 8 (over z, core).
Axes of the slice: x: 2, y: 2, z: 4, core: 2. Of those that a mesh axis runs over, the one named last changes fastest.
Arguments:
- pooled: bfloat16 [8, 512, 32, 256], P('hash', 'group'), may hold values from -0.375 to 0.375
- weight: bfloat16 [1024, 2048], replicated, may hold values from -0.1875 to 0.1875
- cotangent: bfloat16 [8, 512, 2048], P('hash', 'group'), may hold values from -6 to 6
- owners: int32 [8, 32, 512, 2], P('hash', 'group'), may hold values from 0 to 7, all different within a row; in each aligned block of 4096 rows (0 to 4095, 4096 to 8191, ..., all dimensions but the last counted through in order) at most 1365 rows name the same one
- local_rows: int32 [8, 32, 512, 2], P('hash', 'group'), may hold values from 0 to 511
- table: float32 [32, 4096, 256], P('group', 'hash'), may hold values from -0.625 to 0.625
- accum: float32 [32, 4096], P('group', 'hash'), may hold values from 0.05 to 2
Outputs:
- wgrad: bfloat16 [1024, 2048], replicated
- table_out: float32 [32, 4096, 256], P('group', 'hash')
- accum_out: float32 [32, 4096], P('group', 'hash')
Inputs may be any that keep to these rules, and one draw needn't show every extreme that they name: Among the rows of one device (aligned blocks of 4096 bags), no owner is named more than 1365 times, a bound that some block reaches; the 2 owners of one bag differ.
All inputs are finite; a program needn't handle non-finite values.
Results may differ from a plain program's by a relative error of at most 0.0059.
Values may be sent and summed in bfloat16 or wider, within the bound.
No kernel may reach another device: no remote copies, remote signals or barrier semaphores. Data moves between devices by JAX's collectives and lax.ppermute only.
A program may use at most 128 MiB of HBM per device.

v0:
```python
import math
import jax
import jax.numpy as jnp
from jax import lax
from jax.sharding import PartitionSpec as P


def local(pooled, weight, cotangent, owners, local_rows, table, accum):
    vectors = pooled[0]
    samples, feats, width = vectors.shape
    inter = jnp.einsum("sfe,sge->sfg", vectors, vectors, preferred_element_type=jnp.float32).astype(
        jnp.bfloat16
    )
    inter_rows = inter.reshape(samples, feats * feats)
    preact = jnp.dot(inter_rows, weight, preferred_element_type=jnp.float32)
    sigmoid_v = jax.nn.sigmoid(preact)
    dpre = (
        cotangent[0].astype(jnp.float32) * (sigmoid_v * (1.0 + preact * (1.0 - sigmoid_v)))
    ).astype(jnp.bfloat16)
    dinter = lax.dot_general(
        dpre, weight, (((1,), (1,)), ((), ())), preferred_element_type=jnp.float32
    ).reshape(samples, feats, feats)
    dsym = (dinter + jnp.swapaxes(dinter, 1, 2)).astype(jnp.bfloat16)
    dpooled = jnp.einsum("sfg,sge->fse", dsym, vectors, preferred_element_type=jnp.float32).astype(
        jnp.bfloat16
    )
    exchanged = lax.all_to_all(dpooled, "group", split_axis=0, concat_axis=1, tiled=True)
    wlocal = lax.dot_general(
        inter_rows, dpre, (((0,), (0,)), ((), ())), preferred_element_type=jnp.float32
    )
    total_samples = samples * lax.axis_size("group") * lax.axis_size("hash")
    wgrad = (lax.psum(wlocal, ("group", "hash")) / math.sqrt(total_samples)).astype(jnp.bfloat16)
    owner_ids = owners[0]
    row_ids = local_rows[0]
    groups_local, rows_dev = accum.shape
    hashes = lax.axis_size("hash")
    feature_index = jnp.arange(groups_local, dtype=jnp.int32)[:, None, None]
    values = jnp.broadcast_to(exchanged[:, :, None, :], owner_ids.shape + (width,)).reshape(
        -1, width
    )
    dense_keys = (feature_index * (hashes * rows_dev) + owner_ids * rows_dev + row_ids).reshape(-1)
    partial_grad = jax.ops.segment_sum(
        values.astype(jnp.float32), dense_keys, num_segments=groups_local * hashes * rows_dev
    )
    rowgrad = lax.psum_scatter(
        partial_grad.reshape(groups_local, hashes * rows_dev, width).astype(jnp.bfloat16),
        "hash",
        scatter_dimension=1,
        tiled=True,
    ).astype(jnp.float32)
    accum_out = accum + jnp.mean(rowgrad * rowgrad, axis=-1)
    table_out = table - 0.1 * rowgrad / jnp.sqrt(accum_out)[:, :, None]
    return (wgrad, table_out, accum_out)


def solution(mesh):
    in_specs = (
        P("hash", "group", None, None),
        P(),
        P("hash", "group", None),
        P("hash", "group", None, None),
        P("hash", "group", None, None),
        P("group", "hash", None),
        P("group", "hash"),
    )
    out_specs = (P(), P("group", "hash", None), P("group", "hash"))
    return jax.shard_map(local, mesh=mesh, in_specs=in_specs, out_specs=out_specs, check_vma=False)
```

profile of v0, /device:TPU:0, one launch (start us, length us, event | category | flops | bytes accessed | tf_op | source)
XLA Modules:
  0.0 382.3 jit_solution(6259762305518760065)
XLA Ops:
  8.0 0.0 copy-start
  8.0 0.0 all-reduce.2.cloned.1.call-start
  8.1 1.5 copy-done
  9.6 0.7 fusion.11
  10.3 1.1 copy.25
  11.4 0.0 copy-start.2
  11.4 3.0 fusion.27
  14.4 0.0 copy-done.2
  14.4 4.6 %fusion.17 = f32[1024,2048]{1,0:T(8,128)} fusion(bf16[128,1024]{0,1:T(8,128)(2,1)S(1)} %bitcast.47, f32[128,2048]{1,0:T(8,128)S(1)} %fusion.27, bf16[1,128,2048]{2,1,0:T(8,128)(2,1)S(1)} %copy-done.2), kind=kOutput, calls=%fused_computation.19 | convolution fusion | flops 539492352 | bytes 10223616 | tf_op jit(solution)/shard_map/dot_general | solution.py:28
  18.9 0.0 all-reduce.2.cloned.1.call-update
  19.0 3.7 fusion.15
  22.7 0.3 fusion.21
  23.0 1.4 copy.30
  24.5 0.7 convert_bitcast_fusion.1
  25.1 0.0 copy-start.4
  25.2 2.6 copy.31
  27.7 5.1 %all-to-all-start = ((bf16[32,128,256]{2,1,0:T(8,128)(2,1)}), bf16[32,128,256]{2,1,0:T(8,128)(2,1)S(1)}, u32[]{:S(2)}, u32[]{:S(2)}) async-start(bf16[32,128,256]{2,1,0:T(8,128)(2,1)} %copy.31), calls=%async_computation | async-start | bytes 4194304 | tf_op jit(solution)/shard_map/all_to_all | solution.py:27
  32.9 0.0 reduce-scatter.2.cloned.1.call-start
  32.9 0.0 copy-done.4
  32.9 0.0 copy-start.3
  32.9 2.0 copy.26
  34.9 3.1 mul.48
  38.0 1.5 add.47
  39.6 3.0 add.48
  42.6 0.0 copy-done.3
  42.6 2.0 copy.27
  44.6 3.0 squeeze.9
  47.7 20.9 %all-to-all-done = bf16[32,128,256]{2,1,0:T(8,128)(2,1)S(1)} async-done(((bf16[32,128,256]{2,1,0:T(8,128)(2,1)}), bf16[32,128,256]{2,1,0:T(8,128)(2,1)S(1)}, u32[]{:S(2)}, u32[]{:S(2)}) %all-to-all-start) | async-done | bytes 2097184 | tf_op jit(solution)/shard_map/all_to_all | solution.py:27
  68.6 0.5 convert_bitcast_fusion
  69.1 0.4 copy.32
  69.6 4.5 %broadcast_in_dim.5 = f32[8,512,2,256]{3,2,1,0:T(2,128)} broadcast(f32[8,512,256]{2,1,0:T(8,128)S(1)} %bitcast.44), dimensions={0,1,3} | broadcast | bytes 12582912 | tf_op jit(solution)/shard_map/broadcast_in_dim | solution.py:38
  74.0 11.1 %reshape.73 = f32[8192,256]{1,0:T(8,128)} reshape(f32[8,512,2,256]{3,2,1,0:T(2,128)} %broadcast_in_dim.5) | data formatting | bytes 16777216 | tf_op jit(solution)/shard_map/convert_element_type | solution.py:43
  85.2 58.1 %scatter_custom_fusion = f32[32768,256]{1,0:T(8,128)} fusion(s32[8192]{0:T(1024)S(1)} %bitcast.49, f32[8192,256]{1,0:T(8,128)} %reshape.73, f32[]{:T(128)} %constant.3.clone.1), kind=kCustom, calls=%fused_computation.1 | custom fusion | flops 2097152 | bytes 33554944 | tf_op jit(solution)/shard_map/scatter-add | solution.py:42
  143.3 17.5 %convert_element_type.62 = bf16[32768,256]{1,0:T(8,128)(2,1)} convert(f32[32768,256]{1,0:T(8,128)} %scatter_custom_fusion) | non-fusion elementwise | flops 8388608 | bytes 50331648 | tf_op jit(solution)/shard_map/convert_element_type | solution.py:46
  160.7 0.0 reduce-scatter.2.cloned.1.call-update
  160.8 0.0 copy-start.5
  160.8 115.0 %all-reduce.2.cloned.1.call-done = f32[1024,2048]{1,0:T(8,128)} async-done(((f32[1024,2048]{1,0:T(8,128)}), f32[1024,2048]{1,0:T(8,128)}) %all-reduce.2.cloned.1.call-update) | async-done | bytes 8388624 | tf_op jit(solution)/shard_map/psum | solution.py:32
  275.7 6.6 %multiply_convert_fusion = bf16[1024,2048]{1,0:T(8,128)(2,1)} fusion(f32[1024,2048]{1,0:T(8,128)} %all-reduce.2.cloned.1.call-done), kind=kLoop, calls=%fused_computation.3 | loop fusion | flops 4194304 | bytes 12582912 | tf_op jit(solution)/shard_map/convert_element_type | solution.py:32
  282.3 85.0 %reduce-scatter.2.cloned.1.call-done = bf16[8,512,256]{2,1,0:T(8,128)(2,1)} async-done(((bf16[8,4096,256]{2,1,0:T(8,128)(2,1)}), bf16[8,512,256]{2,1,0:T(8,128)(2,1)}) %reduce-scatter.2.cloned.1.call-update) | async-done | bytes 2097168 | tf_op jit(solution)/shard_map/reduce_scatter | solution.py:45
  367.4 2.2 fusion.4
  369.6 0.0 copy-done.5
  369.6 0.6 fusion.26
  370.2 0.0 copy-start.1
  370.2 4.6 %fusion.3 = f32[8,512,256]{2,1,0:T(8,128)} fusion(f32[8,512,256]{2,1,0:T(8,128)} %param.12, bf16[8,512,256]{2,1,0:T(8,128)(2,1)} %reduce-scatter.2.cloned.1.call-done, f32[8,512]{1,0:T(8,128)S(1)} %get-tuple-element.3), kind=kLoop, calls=%fused_computation.7 | loop fusion | flops 4194304 | bytes 10502144 | tf_op jit(solution)/shard_map/sub | solution.py:52
  374.8 0.0 copy-done.1
  (3 shorter events, 0.1 us)
Async XLA Ops:
  8.0 1.6 copy-start
  8.0 267.7 %all-reduce.2.cloned.1.call-start = ((), (), s32[]{:S(2)}) async-start(), calls=%async_computation.2 | async-start | bytes 16777216 | tf_op jit(solution)/shard_map/psum | solution.py:32
  11.4 3.0 copy-start.2
  25.1 7.7 %copy-start.4 = (s32[1,8,512,2]{2,3,1,0:T(2,128)S(1)}, s32[1,8,512,2]{2,3,1,0:T(2,128)}, u32[]{:S(2)}) copy-start(s32[1,8,512,2]{2,3,1,0:T(2,128)} %param.10) | copy-start | bytes 98308
  27.7 40.9 %all-to-all-start = ((bf16[32,128,256]{2,1,0:T(8,128)(2,1)}), bf16[32,128,256]{2,1,0:T(8,128)(2,1)S(1)}, u32[]{:S(2)}, u32[]{:S(2)}) async-start(bf16[32,128,256]{2,1,0:T(8,128)(2,1)} %copy.31), calls=%async_computation | async-start | bytes 4194304 | tf_op jit(solution)/shard_map/all_to_all | solution.py:27
  32.9 334.5 %reduce-scatter.2.cloned.1.call-start = ((), (), s32[]{:S(2)}) async-start(), calls=%async_computation.3 | async-start | bytes 18874368 | tf_op jit(solution)/shard_map/reduce_scatter | solution.py:45
  32.9 9.7 %copy-start.3 = (s32[1,8,512,2]{2,3,1,0:T(2,128)S(1)}, s32[1,8,512,2]{2,3,1,0:T(2,128)}, u32[]{:S(2)}) copy-start(s32[1,8,512,2]{2,3,1,0:T(2,128)} %param.11) | copy-start | bytes 98308
  160.8 208.8 %copy-start.5 = (f32[8,512]{1,0:T(8,128)S(1)}, f32[8,512]{1,0:T(8,128)}, u32[]{:S(2)}) copy-start(f32[8,512]{1,0:T(8,128)} %param.13) | copy-start | bytes 49156
  370.2 4.6 %copy-start.1 = (bf16[1,128,32,256]{3,2,1,0:T(8,128)(2,1)S(1)}, bf16[1,128,32,256]{3,2,1,0:T(8,128)(2,1)}, u32[]{:S(2)}) copy-start(bf16[1,128,32,256]{3,2,1,0:T(8,128)(2,1)} %param.7) | copy-start | bytes 6291460
Sparse Core Ops, SparseCore 0:
  19.1 256.6 all-reduce.1
Sparse Core Ops, SparseCore 1:
  160.8 206.5 reduce-scatter.1
where the time goes:
time: 383 us; the launch traced here: 382 us
  waiting for transfers between devices  221 us (58%)
  other arithmetic  90.5 us (24%)
  local copies, waits for them, and re-layouts  37.4 us (10%)
  between operations  15.6 us (4%)
  matrix products  12.6 us (3%)
  starting transfers between devices  5.15 us (1%)
    psum x1, waiting for transfers between devices, local(): lax.psum(wlocal, ('group', 'hash')) / math.sqrt(total_samples)  115 us
    reduce_scatter x1, waiting for transfers between devices, local(): lax.psum_scatter(partial_grad.reshape(groups_local, hashes * rows_dev, wi...  85 us
    scatter-add x1, other arithmetic, local(): jax.ops.segment_sum(values.astype(jnp.float32), dense_keys, num_segments=...  58.1 us
    all_to_all x1, waiting for transfers between devices, local(): lax.all_to_all(dpooled, 'group', split_axis=0, concat_axis=1, tiled=True)  20.9 us
    convert_element_type x1, other arithmetic, local(): partial_grad.reshape(groups_local, hashes * rows_dev, width)  17.5 us
    convert_element_type x2, local copies, waits for them, and re-layouts, local(): values.astype(jnp.float32)  11.6 us
  transfers between devices with their start and end apart: 3, of which 3 were waited for; matrix products, arithmetic and copies ran while one was open for 32% of the time, Pallas kernels for 0%

commit v1 on v0

--- a/solution.py
+++ b/solution.py
@@ -29,7 +29,13 @@
         inter_rows, dpre, (((0,), (0,)), ((), ())), preferred_element_type=jnp.float32
     )
     total_samples = samples * lax.axis_size("group") * lax.axis_size("hash")
-    wgrad = (lax.psum(wlocal, ("group", "hash")) / math.sqrt(total_samples)).astype(jnp.bfloat16)
+
+    def divide_strings_on(xs):
+        q_next = jax.lax.psum(xs, "group")
+        left_arr = jax.lax.psum(q_next, "hash")
+        return left_arr
+
+    wgrad = (divide_strings_on(wlocal) / math.sqrt(total_samples)).astype(jnp.bfloat16)
     owner_ids = owners[0]
     row_ids = local_rows[0]
     groups_local, rows_dev = accum.shape

time: 383 us -> 557 us (1.45)
  waiting for transfers between devices: 221 us -> 398 us
    psum x1 -> x2, waiting for transfers between devices: 115 us -> 224 us  [the longest x1 175 us: divide_strings_on(): q_next = jax.lax.psum(xs, 'group')]
    reduce_scatter x1, waiting for transfers between devices: 85 us -> 164 us  [local(): lax.psum_scatter(partial_grad.reshape(groups_local, hashes * rows_dev, wi...]
    all_to_all x1, waiting for transfers between devices: 20.9 us -> 9.92 us  [local(): lax.all_to_all(dpooled, 'group', split_axis=0, concat_axis=1, tiled=True)]
  transfers between devices with their start and end apart: 3 -> 4, of which waited for: 3 -> 4; matrix products, arithmetic and copies ran while one was open for 32% -> 22% of each run, Pallas kernels for 0% -> 0%
where the time goes in v1:
time: 557 us; the launch traced here: 556 us
  waiting for transfers between devices  398 us (71%)
  other arithmetic  90.3 us (16%)
  local copies, waits for them, and re-layouts  37.2 us (7%)
  between operations  13.9 us (2%)
  matrix products  12.6 us (2%)
    psum x1, waiting for transfers between devices, divide_strings_on(): q_next = jax.lax.psum(xs, 'group')  175 us
    reduce_scatter x1, waiting for transfers between devices, local(): lax.psum_scatter(partial_grad.reshape(groups_local, hashes * rows_dev, wi...  164 us
    scatter-add x1, other arithmetic, local(): jax.ops.segment_sum(values.astype(jnp.float32), dense_keys, num_segments=...  58.1 us
    psum x1, waiting for transfers between devices, divide_strings_on(): left_arr = jax.lax.psum(q_next, 'hash')  49.4 us
    convert_element_type x1, other arithmetic, local(): partial_grad.reshape(groups_local, hashes * rows_dev, width)  17.3 us
    convert_element_type x2, local copies, waits for them, and re-layouts, local(): values.astype(jnp.float32)  11.5 us
  transfers between devices with their start and end apart: 4, of which 4 were waited for; matrix products, arithmetic and copies ran while one was open for 22% of the time, Pallas kernels for 0%

profile of v1, /device:TPU:0, one launch (start us, length us, event | category | flops | bytes accessed | tf_op | source)
XLA Modules:
  0.0 556.4 jit_solution(6411775365708089196)
XLA Ops:
  7.2 0.0 copy-start
  7.2 0.0 all-reduce.3.cloned.1.call-start
  7.2 1.5 copy-done
  8.8 0.7 fusion.11
  9.4 1.1 copy.25
  10.5 0.0 copy-start.2
  10.5 3.0 fusion.27
  13.5 0.0 copy-done.2
  13.5 4.6 fusion.17
  18.1 0.0 all-reduce.3.cloned.1.call-update
  18.1 0.0 all-reduce.5.cloned.1.call-start
  18.2 174.9 %all-reduce.3.cloned.1.call-done = f32[1024,2048]{1,0:T(8,128)} async-done(((f32[1024,2048]{1,0:T(8,128)}), f32[1024,2048]{1,0:T(8,128)}) %all-reduce.3.cloned.1.call-update) | async-done | bytes 8388624 | tf_op jit(solution)/shard_map/psum | solution.py:34
  193.1 0.0 all-reduce.5.cloned.1.call-update
  193.1 3.7 fusion.15
  196.8 0.3 fusion.21
  197.1 1.4 copy.30
  198.6 0.7 convert_bitcast_fusion.1
  199.3 0.0 copy-start.4
  199.3 2.5 copy.31
  201.8 3.6 all-to-all-start
  205.4 0.2 reduce-scatter.2.cloned.1.call-start
  205.6 0.0 copy-done.4
  205.7 0.0 copy-start.3
  205.7 2.0 copy.26
  207.7 3.1 mul.48
  210.8 1.5 add.49
  212.3 3.0 add.50
  215.3 0.0 copy-done.3
  215.3 2.0 copy.27
  217.3 3.0 squeeze.9
  220.4 9.9 %all-to-all-done = bf16[32,128,256]{2,1,0:T(8,128)(2,1)S(1)} async-done(((bf16[32,128,256]{2,1,0:T(8,128)(2,1)}), bf16[32,128,256]{2,1,0:T(8,128)(2,1)S(1)}, u32[]{:S(2)}, u32[]{:S(2)}) %all-to-all-start) | async-done | bytes 2097184 | tf_op jit(solution)/shard_map/all_to_all | solution.py:27
  230.3 0.5 convert_bitcast_fusion
  230.9 0.4 copy.32
  231.3 4.5 broadcast_in_dim.5
  235.8 11.0 %reshape.73 = f32[8192,256]{1,0:T(8,128)} reshape(f32[8,512,2,256]{3,2,1,0:T(2,128)} %broadcast_in_dim.5) | data formatting | bytes 16777216 | tf_op jit(solution)/shard_map/convert_element_type | solution.py:49
  246.8 58.1 %scatter_custom_fusion = f32[32768,256]{1,0:T(8,128)} fusion(s32[8192]{0:T(1024)S(1)} %bitcast.49, f32[8192,256]{1,0:T(8,128)} %reshape.73, f32[]{:T(128)} %constant.3.clone.1), kind=kCustom, calls=%fused_computation.1 | custom fusion | flops 2097152 | bytes 33554944 | tf_op jit(solution)/shard_map/scatter-add | solution.py:48
  304.9 17.3 %convert_element_type.62 = bf16[32768,256]{1,0:T(8,128)(2,1)} convert(f32[32768,256]{1,0:T(8,128)} %scatter_custom_fusion) | non-fusion elementwise | flops 8388608 | bytes 50331648 | tf_op jit(solution)/shard_map/convert_element_type | solution.py:52
  322.2 0.0 reduce-scatter.2.cloned.1.call-update
  322.3 0.0 copy-start.5
  322.3 49.4 %all-reduce.5.cloned.1.call-done = f32[1024,2048]{1,0:T(8,128)} async-done(((f32[1024,2048]{1,0:T(8,128)}), f32[1024,2048]{1,0:T(8,128)}) %all-reduce.5.cloned.1.call-update) | async-done | bytes 8388624 | tf_op jit(solution)/shard_map/psum | solution.py:35
  371.7 6.5 %multiply_convert_fusion = bf16[1024,2048]{1,0:T(8,128)(2,1)} fusion(f32[1024,2048]{1,0:T(8,128)} %all-reduce.5.cloned.1.call-done), kind=kLoop, calls=%fused_computation.3 | loop fusion | flops 4194304 | bytes 12582912 | tf_op jit(solution)/shard_map/convert_element_type | solution.py:38
  378.2 164.1 %reduce-scatter.2.cloned.1.call-done = bf16[8,512,256]{2,1,0:T(8,128)(2,1)} async-done(((bf16[8,4096,256]{2,1,0:T(8,128)(2,1)}), bf16[8,512,256]{2,1,0:T(8,128)(2,1)}) %reduce-scatter.2.cloned.1.call-update) | async-done | bytes 2097168 | tf_op jit(solution)/shard_map/reduce_scatter | solution.py:51
  542.4 2.2 fusion.4
  544.6 0.0 copy-done.5
  544.6 0.6 fusion.26
  545.2 0.0 copy-start.1
  545.2 4.6 fusion.3
  549.8 0.0 copy-done.1
  (3 shorter events, 0.1 us)
Async XLA Ops:
  7.2 1.6 copy-start
  7.2 185.9 %all-reduce.3.cloned.1.call-start = ((), (), s32[]{:S(2)}) async-start(), calls=%async_computation.2 | async-start | bytes 16777216 | tf_op jit(solution)/shard_map/psum | solution.py:34
  10.5 3.0 copy-start.2
  18.1 353.5 %all-reduce.5.cloned.1.call-start = ((), (), s32[]{:S(2)}) async-start(), calls=%async_computation.3 | async-start | bytes 16777216 | tf_op jit(solution)/shard_map/psum | solution.py:35
  199.3 6.4 %copy-start.4 = (s32[1,8,512,2]{2,3,1,0:T(2,128)S(1)}, s32[1,8,512,2]{2,3,1,0:T(2,128)}, u32[]{:S(2)}) copy-start(s32[1,8,512,2]{2,3,1,0:T(2,128)} %param.10) | copy-start | bytes 98308
  201.8 28.6 %all-to-all-start = ((bf16[32,128,256]{2,1,0:T(8,128)(2,1)}), bf16[32,128,256]{2,1,0:T(8,128)(2,1)S(1)}, u32[]{:S(2)}, u32[]{:S(2)}) async-start(bf16[32,128,256]{2,1,0:T(8,128)(2,1)} %copy.31), calls=%async_computation | async-start | bytes 4194304 | tf_op jit(solution)/shard_map/all_to_all | solution.py:27
  205.4 337.0 %reduce-scatter.2.cloned.1.call-start = ((), (), s32[]{:S(2)}) async-start(), calls=%async_computation.4 | async-start | bytes 18874368 | tf_op jit(solution)/shard_map/reduce_scatter | solution.py:51
  205.7 9.7 %copy-start.3 = (s32[1,8,512,2]{2,3,1,0:T(2,128)S(1)}, s32[1,8,512,2]{2,3,1,0:T(2,128)}, u32[]{:S(2)}) copy-start(s32[1,8,512,2]{2,3,1,0:T(2,128)} %param.11) | copy-start | bytes 98308
  322.3 222.3 %copy-start.5 = (f32[8,512]{1,0:T(8,128)S(1)}, f32[8,512]{1,0:T(8,128)}, u32[]{:S(2)}) copy-start(f32[8,512]{1,0:T(8,128)} %param.13) | copy-start | bytes 49156
  545.2 4.6 copy-start.1
Sparse Core Ops, SparseCore 0:
  18.3 174.7 all-reduce.2
  195.4 176.2 all-reduce.4
  374.0 168.2 reduce-scatter.1
